TPU v7x, 512 devices: a whole 4x4x16 slice. The times are simulated.
512 devices in a mesh: seq: 64 (over z, y), tp: 8 (over x, core).
Axes of the slice: x: 4, y: 4, z: 16, core: 2. Of those that a mesh axis runs over, the one named last changes fastest.
Arguments:
- hidden: bfloat16 [384, 2048], P(None, 'seq'), may hold values from -12 to 12
- ln1_gain: float32 [2048], P('seq'), may hold values from 0.1 to 1.9
- wq: bfloat16 [2048, 2048], P('seq', 'tp'), may hold values from -0.125 to 0.125
- wk: bfloat16 [2048, 1024], P('seq', 'tp'), may hold values from -0.125 to 0.125
- wv: bfloat16 [2048, 1024], P('seq', 'tp'), may hold values from -0.125 to 0.125
- wg: bfloat16 [2048, 2048], P('seq', 'tp'), may hold values from -0.125 to 0.125
- q_gain: float32 [128], replicated, may hold values from 1 to 30
- key_gain: float32 [128], replicated, may hold values from 0.5 to 1.5
- wo: bfloat16 [2048, 2048], P('tp', 'seq'), may hold values from -0.5 to 0.5
- ln2_gain: float32 [2048], P('seq'), may hold values from 0.1 to 1.9
- w_gate: bfloat16 [2048, 6144], P('seq', 'tp'), may hold values from -0.125 to 0.125
- w_up: bfloat16 [2048, 6144], P('seq', 'tp'), may hold values from -0.125 to 0.125
- w_down: bfloat16 [6144, 2048], P('tp', 'seq'), may hold values from -0.078125 to 0.078125
- last_gain: float32 [2048], P('seq'), may hold values from 0.1 to 1.9
- head_weight: bfloat16 [2048, 131072], P(None, ('seq', 'tp')), may hold values from -0.125 to 0.125
- inv_temp: float32 [8], replicated, may hold values from 0.5 to 64
- key_cache: bfloat16 [8, 16384, 1024], P(None, 'seq', 'tp'), may hold values from -40 to 40
- value_cache: bfloat16 [8, 16384, 1024], P(None, 'seq', 'tp'), may hold values from -6 to 6
- lengths: int32 [8], replicated, may hold values from 1 to 16336
- parents: int32 [8, 48], replicated, may hold values from 0 to 46, as said below
- accepted: int32 [8], replicated, may hold values from 0 to 47
Outputs:
- logprobs: float32 [384, 131072], P(None, ('seq', 'tp'))
- next_hidden: bfloat16 [384, 2048], P(None, 'seq')
- updated_key_cache: bfloat16 [8, 16384, 1024], P(None, 'seq', 'tp')
- updated_value_cache: bfloat16 [8, 16384, 1024], P(None, 'seq', 'tp')
Inputs may be any that keep to these rules, and one draw needn't show every extreme that they name: parents[r, 0] = 0; for i >= 1, i - 4 <= parents[r, i] < i.
All inputs are finite; a program needn't handle non-finite values.
Results may differ from a plain program's by a relative error of at most 0.012.
Values may be sent and summed in bfloat16 or wider, within the bound.
No kernel may reach another device: no remote copies, remote signals or barrier semaphores. Data moves between devices by JAX's collectives and lax.ppermute only.
A program may use at most 128 MiB of HBM per device.

v0:
```python
import jax
import jax.numpy as jnp
from jax import lax
from jax.sharding import PartitionSpec as P

EPSILON = 1e-06
ROPE_BASE = 1000000.0
NEGATIVE = -1e30


def ancestry(parents):
    node_count = parents.shape[-1]
    node_ids = jnp.arange(node_count, dtype=jnp.int32)
    reachable = (parents[..., :, None] == node_ids[None, :]).astype(jnp.float32)
    reachable = jnp.maximum(reachable, jnp.eye(node_count, dtype=jnp.float32))
    for turn in range((node_count - 1).bit_length()):
        reachable = jnp.minimum(
            jnp.einsum("rij,rjk->rik", reachable, reachable, precision=lax.Precision.HIGHEST), 1.0
        )
    return reachable


def head_norm(values, gain):
    meansq = jnp.mean(values * values, axis=-1, keepdims=True)
    return values * lax.rsqrt(meansq + EPSILON) * gain


def apply_rotary(values, places):
    half_dim = values.shape[-1] // 2
    spread = ROPE_BASE ** (-jnp.arange(half_dim, dtype=jnp.float32) / half_dim)
    angles = places.astype(jnp.float32)[:, None] * spread[None, :]
    cosine = jnp.cos(angles)[:, None, :]
    sine = jnp.sin(angles)[:, None, :]
    lower_part = values[..., :half_dim]
    upper_part = values[..., half_dim:]
    return jnp.concatenate(
        [lower_part * cosine - upper_part * sine, upper_part * cosine + lower_part * sine], axis=-1
    )


def cache_part(query_blocks, key_block, value_block, valid_slot):
    scores = jnp.einsum(
        "rikgd,rckd->rkgic", query_blocks, key_block, preferred_element_type=jnp.float32
    )
    valid_slot = valid_slot[:, None, None, None, :]
    row_peak = jnp.max(jnp.where(valid_slot, scores, NEGATIVE), axis=-1)
    weights = jnp.where(valid_slot, jnp.exp(scores - row_peak[..., None]), 0.0)
    row_mass = jnp.sum(weights, axis=-1)
    weighted = jnp.einsum(
        "rkgic,rckd->rkgid",
        weights.astype(jnp.bfloat16),
        value_block,
        preferred_element_type=jnp.float32,
    )
    return (row_peak, row_mass, weighted)


def on_device(
    hidden,
    ln1_gain,
    wq,
    wk,
    wv,
    wg,
    q_gain,
    key_gain,
    wo,
    ln2_gain,
    w_gate,
    w_up,
    w_down,
    last_gain,
    head_weight,
    inv_temp,
    key_cache,
    value_cache,
    lengths,
    parents,
    accepted,
):
    seq_count = lax.axis_size("seq")
    model_width = hidden.shape[1] * seq_count
    head_dim = q_gain.shape[0]
    query_heads = wq.shape[1] // head_dim
    kv_heads = wk.shape[1] // head_dim
    query_group_size = query_heads // kv_heads
    requests, tree_size = parents.shape
    token_count = hidden.shape[0]
    slot_count = key_cache.shape[1]
    slot_start = lax.axis_index("seq") * slot_count
    parent_links = ancestry(parents)
    tree_node_depth = jnp.sum((parent_links > 0.5).astype(jnp.int32), axis=-1) - 1
    token_position = (lengths[:, None] + tree_node_depth).reshape(-1)
    hidden_wide = hidden.astype(jnp.float32)
    squares = lax.psum(jnp.sum(hidden_wide * hidden_wide, axis=1), "seq")
    normed1 = (hidden_wide * lax.rsqrt(squares / model_width + EPSILON)[:, None] * ln1_gain).astype(
        jnp.bfloat16
    )
    q_sum, key_sum, v_sum, gate = lax.psum(
        (
            jnp.dot(normed1, wq, preferred_element_type=jnp.float32),
            jnp.dot(normed1, wk, preferred_element_type=jnp.float32),
            jnp.dot(normed1, wv, preferred_element_type=jnp.float32),
            jnp.dot(normed1, wg, preferred_element_type=jnp.float32),
        ),
        "seq",
    )
    query_rows_all = apply_rotary(
        head_norm(q_sum.reshape(token_count, query_heads, head_dim), q_gain), token_position
    ) * head_dim ** (-0.5)
    query_rows_all = query_rows_all.astype(jnp.bfloat16).reshape(
        requests, tree_size, kv_heads, query_group_size, head_dim
    )
    draft_keys = apply_rotary(
        head_norm(key_sum.reshape(token_count, kv_heads, head_dim), key_gain), token_position
    ).astype(jnp.bfloat16)
    draft_values = v_sum.astype(jnp.bfloat16)
    tree_keys = draft_keys.reshape(requests, tree_size, kv_heads, head_dim)
    tree_values = draft_values.reshape(requests, tree_size, kv_heads, head_dim)
    cache_keys = key_cache.reshape(requests, slot_count, kv_heads, head_dim)
    cache_values = value_cache.reshape(requests, slot_count, kv_heads, head_dim)
    slot_ids = slot_start + jnp.arange(slot_count, dtype=jnp.int32)
    local_state = cache_part(
        query_rows_all, cache_keys, cache_values, slot_ids[None, :] < lengths[:, None]
    )
    local_peak, local_mass, local_sum = local_state
    cache_peak = lax.pmax(local_peak, "seq")
    factor = jnp.exp(local_peak - cache_peak)
    cache_mass, cache_sum = lax.psum((local_mass * factor, local_sum * factor[..., None]), "seq")
    tree_scores = jnp.einsum(
        "rikgd,rjkd->rkgij", query_rows_all, tree_keys, preferred_element_type=jnp.float32
    )
    valid_node = (parent_links > 0.5)[:, None, None, :, :]
    row_top = jnp.maximum(
        cache_peak, jnp.max(jnp.where(valid_node, tree_scores, NEGATIVE), axis=-1)
    )
    tree_weights = jnp.where(valid_node, jnp.exp(tree_scores - row_top[..., None]), 0.0)
    cache_factor = jnp.exp(cache_peak - row_top)
    row_mass = cache_mass * cache_factor + jnp.sum(tree_weights, axis=-1)
    weighted = cache_sum * cache_factor[..., None] + jnp.einsum(
        "rkgij,rjkd->rkgid",
        tree_weights.astype(jnp.bfloat16),
        tree_values,
        preferred_element_type=jnp.float32,
    )
    attention_result = jnp.transpose(weighted / row_mass[..., None], (0, 3, 1, 2, 4)).reshape(
        token_count, query_heads * head_dim
    )
    gated = (attention_result * jax.nn.sigmoid(gate)).astype(jnp.bfloat16)
    attn_sum = lax.psum(jnp.dot(gated, wo, preferred_element_type=jnp.float32), "tp")
    middle = (hidden_wide + attn_sum).astype(jnp.bfloat16)
    middle_wide = middle.astype(jnp.float32)
    squares_mid = lax.psum(jnp.sum(middle_wide * middle_wide, axis=1), "seq")
    normed2 = (
        middle_wide * lax.rsqrt(squares_mid / model_width + EPSILON)[:, None] * ln2_gain
    ).astype(jnp.bfloat16)
    gate_part, up_part = lax.psum(
        (
            jnp.dot(normed2, w_gate, preferred_element_type=jnp.float32),
            jnp.dot(normed2, w_up, preferred_element_type=jnp.float32),
        ),
        "seq",
    )
    activated = (jax.nn.silu(gate_part) * up_part).astype(jnp.bfloat16)
    down_part = jnp.dot(activated, w_down, preferred_element_type=jnp.float32)
    down_sum = lax.psum(down_part, "tp")
    next_hidden = (middle_wide + down_sum).astype(jnp.bfloat16)
    next_wide = next_hidden.astype(jnp.float32)
    squares_last = lax.psum(jnp.sum(next_wide * next_wide, axis=1), "seq")
    normed3 = (
        next_wide * lax.rsqrt(squares_last / model_width + EPSILON)[:, None] * last_gain
    ).astype(jnp.bfloat16)
    logits = jnp.dot(
        lax.all_gather(normed3, "seq", axis=1, tiled=True),
        head_weight,
        preferred_element_type=jnp.float32,
    )
    logits = logits * jnp.repeat(inv_temp, tree_size)[:, None]
    vocab_top = lax.pmax(jnp.max(logits, axis=1), ("seq", "tp"))
    vocab_total = lax.psum(jnp.sum(jnp.exp(logits - vocab_top[:, None]), axis=1), ("seq", "tp"))
    logprobs = logits - (vocab_top + jnp.log(vocab_total))[:, None]
    accepted_rows = parent_links[jnp.arange(requests), accepted]
    target = token_position.reshape(requests, tree_size)
    slot_all = slot_start + jnp.arange(slot_count, dtype=jnp.int32)
    placed = (slot_all[None, :, None] == target[:, None, :]).astype(jnp.float32) * accepted_rows[
        :, None, :
    ]
    hits = (jnp.sum(placed, axis=2) > 0.5)[:, :, None]
    placed_low = placed.astype(jnp.bfloat16)
    moved_keys = jnp.einsum(
        "rca,rae->rce",
        placed_low,
        draft_keys.reshape(requests, tree_size, kv_heads * head_dim),
        preferred_element_type=jnp.float32,
    ).astype(jnp.bfloat16)
    moved_values = jnp.einsum(
        "rca,rae->rce",
        placed_low,
        draft_values.reshape(requests, tree_size, kv_heads * head_dim),
        preferred_element_type=jnp.float32,
    ).astype(jnp.bfloat16)
    updated_key_cache = jnp.where(hits, moved_keys, key_cache)
    updated_value_cache = jnp.where(hits, moved_values, value_cache)
    return (logprobs, next_hidden, updated_key_cache, updated_value_cache)


def solution(mesh):
    in_specs = (
        P(None, "seq"),
        P("seq"),
        P("seq", "tp"),
        P("seq", "tp"),
        P("seq", "tp"),
        P("seq", "tp"),
        P(),
        P(),
        P("tp", "seq"),
        P("seq"),
        P("seq", "tp"),
        P("seq", "tp"),
        P("tp", "seq"),
        P("seq"),
        P(None, ("seq", "tp")),
        P(),
        P(None, "seq", "tp"),
        P(None, "seq", "tp"),
        P(),
        P(),
        P(),
    )
    out_specs = (P(None, ("seq", "tp")), P(None, "seq"), P(None, "seq", "tp"), P(None, "seq", "tp"))
    return jax.shard_map(
        on_device, mesh=mesh, in_specs=in_specs, out_specs=out_specs, check_vma=False
    )
```

profile of v0, /device:TPU:1, one launch (start us, length us, event | category | flops | bytes accessed | tf_op | source)
XLA Modules:
  0.0 1792.0 jit_solution(4256023891018787633)
XLA Ops:
  7.2 0.8 fusion.51
  8.1 122.9 %psum.98 = f32[384]{0:T(512)S(1)} all-reduce(f32[384]{0:T(512)S(1)} %fusion.51), channel_id=1, replica_groups=mesh['seq'=64,'tp'=8] {'seq'}, use_global_device_ids=true, to_apply=%region_1.0 | all-reduce | flops 384 | bytes 3072 | tf_op jit(solution)/shard_map/psum | solution.py:95
  130.9 1.8 fusion.88
  132.8 1.4 convolution_minimum_fusion.5
  136.2 1.0 fusion.86
  137.7 1.1 fusion.82
  138.7 269.0 %all-reduce.8.cloned.1.call-done = f32[384,2,128]{0,2,1:T(8,128)} async-done(((f32[384,2,128]{0,2,1:T(8,128)}), f32[384,2,128]{0,2,1:T(8,128)}) %all-reduce.8.cloned.1.call-update) | async-done | bytes 393232 | tf_op jit(solution)/shard_map/psum | solution.py:99
  407.7 1.0 multiply_reduce_fusion
  408.8 1.1 multiply_multiply_fusion
  411.8 114.2 %pmax.14 = f32[8,1,2,48]{3,2,0,1:T(2,128)S(1)} all-reduce(f32[8,1,2,48]{3,2,0,1:T(2,128)S(1)} %bitcast.134), channel_id=1, replica_groups=mesh['seq'=64,'tp'=8] {'seq'}, use_global_device_ids=true, to_apply=%region_6.0 | all-reduce | flops 768 | bytes 6144 | tf_op jit(solution)/shard_map/pmax | solution.py:127
  526.5 1.1 fusion.2
  528.0 219.4 %all-reduce.13 = (bf16[384,128]{1,0:T(8,128)(2,1)S(1)}, f32[8,1,2,48]{3,2,0,1:T(2,128)S(1)}) all-reduce(f32[384,128]{1,0:T(8,128)S(1)} %fusion.84, f32[8,1,2,48]{3,2,0,1:T(2,128)S(1)} %get-tuple-element.32), channel_id=1, replica_groups=mesh['seq'=64,'tp'=8] {'seq'}, use_global_device_ids=true, to_apply=%region_11.12 | all-reduce | flops 49920 | bytes 301056 | tf_op jit(solution)/shard_map/psum | solution.py:99
  747.3 74.5 %all-reduce.12.cloned.1.call-done = (f32[8,1,2,48,128]{4,3,2,0,1:T(8,128)}, f32[384,128]{1,0:T(8,128)}, f32[384,256]{1,0:T(8,128)}) async-done(((f32[8,1,2,48,128]{4,3,2,0,1:T(8,128)}, f32[384,128]{1,0:T(8,128)}, f32[384,256]{1,0:T(8,128)}), (f32[8,1,2,48,128]{4,3,2,0,1:T(8,128)}, f32[384,128]{1,0:T(8,128)}, f32[384,256]{1,0:T(8,128)})) %all-reduce.12.cloned.1.call-update) | async-done | bytes 983056 | tf_op jit(solution)/shard_map/psum | solution.py:129
  821.8 1.1 multiply_reduce_fusion.1
  822.9 1.1 multiply_bitcast_fusion
  824.0 0.8 fusion.25
  826.7 39.8 %psum.105 = f32[384,32]{0,1:T(8,128)S(1)} all-reduce(f32[384,32]{0,1:T(8,128)S(1)} %fusion.43), channel_id=1, replica_groups=mesh['seq'=64,'tp'=8] {'tp'}, use_global_device_ids=true, to_apply=%region_16.17 | all-reduce | flops 12288 | bytes 98304 | tf_op jit(solution)/shard_map/psum | solution.py:150
  866.5 110.1 %psum.106 = f32[384]{0:T(512)S(1)} all-reduce(f32[384]{0:T(512)S(1)} %get-tuple-element.21), channel_id=1, replica_groups=mesh['seq'=64,'tp'=8] {'seq'}, use_global_device_ids=true, to_apply=%region_18.19 | all-reduce | flops 384 | bytes 3072 | tf_op jit(solution)/shard_map/psum | solution.py:153
  976.7 1.4 fusion.63
  978.1 1.4 fusion.65
  979.6 295.4 %all-reduce.10.cloned.1.call-done = (f32[384,768]{1,0:T(8,128)}, f32[384,768]{1,0:T(8,128)}) async-done(((f32[384,768]{1,0:T(8,128)}, f32[384,768]{1,0:T(8,128)}), (f32[384,768]{1,0:T(8,128)}, f32[384,768]{1,0:T(8,128)})) %all-reduce.10.cloned.1.call-update) | async-done | bytes 2359312 | tf_op jit(solution)/shard_map/psum | solution.py:157
  1275.1 2.1 fusion.8
  1277.2 30.1 %psum.109 = f32[384,32]{0,1:T(8,128)S(1)} all-reduce(f32[384,32]{0,1:T(8,128)S(1)} %fusion.8), channel_id=1, replica_groups=mesh['seq'=64,'tp'=8] {'tp'}, use_global_device_ids=true, to_apply=%region_21.22 | all-reduce | flops 12288 | bytes 98304 | tf_op jit(solution)/shard_map/psum | solution.py:166
  1307.3 112.8 %psum.110 = f32[384]{0:T(512)S(1)} all-reduce(f32[384]{0:T(512)S(1)} %get-tuple-element.19), channel_id=1, replica_groups=mesh['seq'=64,'tp'=8] {'seq'}, use_global_device_ids=true, to_apply=%region_23.24 | all-reduce | flops 384 | bytes 3072 | tf_op jit(solution)/shard_map/psum | solution.py:169
  1420.1 0.7 fusion.50
  1421.9 1.7 fusion.1
  1423.5 1.6 fusion
  1425.1 148.8 %all-gather.2.cloned.1.call-done = bf16[384,2048]{0,1:T(8,128)(2,1)} async-done(((bf16[384,32]{0,1:T(8,128)(2,1)}), bf16[384,2048]{0,1:T(8,128)(2,1)}) %all-gather.2.cloned.1.call-update) | async-done | bytes 1572880 | tf_op jit(solution)/shard_map/all_gather | solution.py:174
  1573.9 2.2 fusion.93
  1576.1 109.6 %pmax.15 = f32[384]{0:T(512)S(1)} all-reduce(f32[384]{0:T(512)S(1)} %get-tuple-element.41), channel_id=1, replica_groups=mesh['seq'=64,'tp'=8] {'seq','tp'}, use_global_device_ids=true, to_apply=%region_25.26 | all-reduce | flops 384 | bytes 3072 | tf_op jit(solution)/shard_map/pmax | solution.py:179
  1685.8 98.8 %psum.111 = f32[384]{0:T(512)S(1)} all-reduce(f32[384]{0:T(512)S(1)} %exponential_reduce_fusion), channel_id=1, replica_groups=mesh['seq'=64,'tp'=8] {'seq','tp'}, use_global_device_ids=true, to_apply=%region_27.28 | all-reduce | flops 384 | bytes 3072 | tf_op jit(solution)/shard_map/psum | solution.py:180
  1784.6 0.9 copy.35
  (100 shorter events, 8.2 us)
Async XLA Ops:
  7.2 1566.7 %copy-start = (bf16[2048,256]{1,0:T(8,128)(2,1)S(1)}, bf16[2048,256]{1,0:T(8,128)(2,1)}, u32[]{:S(2)}) copy-start(bf16[2048,256]{1,0:T(8,128)(2,1)} %param.35) | copy-start | bytes 3145732
  7.2 400.6 %all-reduce.8.cloned.1.call-start = ((), (), s32[]{:S(2)}) async-start(), calls=%async_computation | async-start | bytes 786432 | tf_op jit(solution)/shard_map/psum | solution.py:99
  132.7 689.1 %all-reduce.12.cloned.1.call-start = ((), (), s32[]{:S(2)}) async-start(), calls=%async_computation.3 | async-start | bytes 1966080 | tf_op jit(solution)/shard_map/psum | solution.py:129
  134.6 1.4 copy-start.12
  134.6 1.6 copy-start.1
  134.6 1.6 copy-start.8
  134.6 1.6 copy-start.9
  135.0 2.7 copy-start.7
  135.3 273.5 %copy-start.16 = (f32[128]{0:T(128)S(1)}, f32[128]{0:T(128)}, u32[]{:S(2)}) copy-start(f32[128]{0:T(128)} %param.27) | copy-start | bytes 1540
  410.4 1.0 copy-start.2
  411.4 115.0 %copy-start.3 = (bf16[8,256,128]{2,1,0:T(8,128)(2,1)S(1)}, bf16[8,256,128]{2,1,0:T(8,128)(2,1)}, u32[]{:S(2)}) copy-start(bf16[8,256,128]{2,1,0:T(8,128)(2,1)} %param.38) | copy-start | bytes 1572868
  526.5 1.2 copy-start.10
  527.6 295.3 %copy-start.13 = (f32[128]{0:T(128)S(1)}, f32[128]{0:T(128)}, u32[]{:S(2)}) copy-start(f32[128]{0:T(128)} %param.28) | copy-start | bytes 1540
  527.6 747.5 %all-reduce.10.cloned.1.call-start = ((), (), s32[]{:S(2)}) async-start(), calls=%async_computation.2 | async-start | bytes 4718592 | tf_op jit(solution)/shard_map/psum | solution.py:157
  822.9 2.5 copy-start.18
  825.4 1.0 copy-start.17
  825.4 1.0 copy-start.20
  826.0 150.7 %copy-start.5 = (bf16[32,768]{1,0:T(8,128)(2,1)S(1)}, bf16[32,768]{1,0:T(8,128)(2,1)}, u32[]{:S(2)}) copy-start(bf16[32,768]{1,0:T(8,128)(2,1)} %param.32) | copy-start | bytes 147460
  826.0 150.7 %copy-start.11 = (f32[32]{0:T(128)S(1)}, f32[32]{0:T(128)}, u32[]{:S(2)}) copy-start(f32[32]{0:T(128)} %param.30) | copy-start | bytes 388
  826.7 151.5 %copy-start.6 = (bf16[32,768]{1,0:T(8,128)(2,1)S(1)}, bf16[32,768]{1,0:T(8,128)(2,1)}, u32[]{:S(2)}) copy-start(bf16[32,768]{1,0:T(8,128)(2,1)} %param.31) | copy-start | bytes 147460
  979.5 295.5 %copy-start.19 = (bf16[768,32]{0,1:T(8,128)(2,1)S(1)}, bf16[768,32]{0,1:T(8,128)(2,1)}, u32[]{:S(2)}) copy-start(bf16[768,32]{0,1:T(8,128)(2,1)} %param.33) | copy-start | bytes 147460
  979.6 594.3 %all-gather.2.cloned.1.call-start = ((), (), s32[]{:S(2)}) async-start(), calls=%async_computation.1 | async-start | bytes 1597440 | tf_op jit(solution)/shard_map/all_gather | solution.py:174
  1275.0 145.0 %copy-start.14 = (f32[32]{0:T(128)S(1)}, f32[32]{0:T(128)}, u32[]{:S(2)}) copy-start(f32[32]{0:T(128)} %param.34) | copy-start | bytes 388
  1275.0 145.7 %copy-start.15 = (f32[8]{0:T(128)S(1)}, f32[8]{0:T(128)}, u32[]{:S(2)}) copy-start(f32[8]{0:T(128)} %param.36) | copy-start | bytes 100
  1275.0 146.0 %copy-start.21 = (s32[8]{0:T(128)S(1)}, s32[8]{0:T(128)}, u32[]{:S(2)}) copy-start(s32[8]{0:T(128)} %param.41) | copy-start | bytes 100
  1307.3 117.8 %copy-start.4 = (bf16[384,32]{0,1:T(8,128)(2,1)}, bf16[384,32]{0,1:T(8,128)(2,1)S(1)}, u32[]{:S(2)}) copy-start(bf16[384,32]{0,1:T(8,128)(2,1)S(1)} %get-tuple-element.20) | copy-start | bytes 73732
Sparse Core Ops, SparseCore 0:
  132.9 274.8 all-reduce.7
  527.7 294.0 all-reduce.11
  979.7 295.2 all-reduce.9
  1420.9 152.9 all-gather.1
where the time goes:
time: 1790 us
  blocking collectives  958 us (54%)
  waiting for transfers between devices  788 us (44%)
  matrix products  19.9 us (1%)
    psum x1, waiting for transfers between devices, on_device(): lax.psum((jnp.dot(normed2, w_gate, preferred_element_type=jnp.float32), j...  295 us
    psum x1, waiting for transfers between devices, on_device(): lax.psum((jnp.dot(normed1, wq, preferred_element_type=jnp.float32), jnp.d...  269 us
    psum x1, blocking collectives, on_device(): lax.psum((jnp.dot(normed1, wq, preferred_element_type=jnp.float32), jnp.d...  219 us
    all_gather x1, waiting for transfers between devices, on_device(): lax.all_gather(normed3, 'seq', axis=1, tiled=True)  149 us
    psum x1, blocking collectives, on_device(): squares = lax.psum(jnp.sum(hidden_wide * hidden_wide, axis=1), 'seq')  123 us
    pmax x1, blocking collectives, on_device(): cache_peak = lax.pmax(local_peak, 'seq')  114 us
    psum x1, blocking collectives, on_device(): squares_last = lax.psum(jnp.sum(next_wide * next_wide, axis=1), 'seq')  113 us
    psum x1, blocking collectives, on_device(): squares_mid = lax.psum(jnp.sum(middle_wide * middle_wide, axis=1), 'seq')  110 us
  transfers between devices with their start and end apart: 4, of which 4 were waited for; matrix products, arithmetic and copies ran while one was open for 1% of the time, Pallas kernels for 0%

commit v1 on v0

--- a/solution.py
+++ b/solution.py
@@ -177,7 +177,9 @@
     )
     logits = logits * jnp.repeat(inv_temp, tree_size)[:, None]
     vocab_top = lax.pmax(jnp.max(logits, axis=1), ("seq", "tp"))
-    vocab_total = lax.psum(jnp.sum(jnp.exp(logits - vocab_top[:, None]), axis=1), ("seq", "tp"))
+    vocab_total = lax.psum(
+        lax.psum(jnp.sum(jnp.exp(logits - vocab_top[:, None]), axis=1), "seq"), "tp"
+    )
     logprobs = logits - (vocab_top + jnp.log(vocab_total))[:, None]
     accepted_rows = parent_links[jnp.arange(requests), accepted]
     target = token_position.reshape(requests, tree_size)

time: 1790 us -> 1850 us (1.034)
  blocking collectives: 958 us -> 1010 us
    psum x1 -> x2, blocking collectives: 98.8 us -> 152 us  [the longest x1 112 us: on_device(): lax.psum(jnp.sum(jnp.exp(logits - vocab_top[:, None]), axis=1), 'seq')]
where the time goes in v1:
time: 1850 us
  blocking collectives  1010 us (55%)
  waiting for transfers between devices  788 us (43%)
  matrix products  19.9 us (1%)
    psum x1, waiting for transfers between devices, on_device(): lax.psum((jnp.dot(normed2, w_gate, preferred_element_type=jnp.float32), j...  295 us
    psum x1, waiting for transfers between devices, on_device(): lax.psum((jnp.dot(normed1, wq, preferred_element_type=jnp.float32), jnp.d...  269 us
    psum x1, blocking collectives, on_device(): lax.psum((jnp.dot(normed1, wq, preferred_element_type=jnp.float32), jnp.d...  219 us
    all_gather x1, waiting for transfers between devices, on_device(): lax.all_gather(normed3, 'seq', axis=1, tiled=True)  149 us
    psum x1, blocking collectives, on_device(): squares = lax.psum(jnp.sum(hidden_wide * hidden_wide, axis=1), 'seq')  123 us
    pmax x1, blocking collectives, on_device(): cache_peak = lax.pmax(local_peak, 'seq')  114 us
    psum x1, blocking collectives, on_device(): squares_last = lax.psum(jnp.sum(next_wide * next_wide, axis=1), 'seq')  113 us
    psum x1, blocking collectives, on_device(): lax.psum(jnp.sum(jnp.exp(logits - vocab_top[:, None]), axis=1), 'seq')  112 us
  transfers between devices with their start and end apart: 4, of which 4 were waited for; matrix products, arithmetic and copies ran while one was open for 1% of the time, Pallas kernels for 0%

profile of v1, /device:TPU:1, one launch (start us, length us, event | category | flops | bytes accessed | tf_op | source)
XLA Modules:
  0.0 1845.6 jit_solution(5912648984851011739)
XLA Ops:
  7.2 0.8 fusion.51
  8.1 122.9 %psum.105 = f32[384]{0:T(512)S(1)} all-reduce(f32[384]{0:T(512)S(1)} %fusion.51), channel_id=1, replica_groups=mesh['seq'=64,'tp'=8] {'seq'}, use_global_device_ids=true, to_apply=%region_1.0 | all-reduce | flops 384 | bytes 3072 | tf_op jit(solution)/shard_map/psum | solution.py:95
  130.9 1.8 fusion.88
  132.8 1.4 convolution_minimum_fusion.5
  136.2 1.0 fusion.86
  137.7 1.1 fusion.82
  138.7 269.0 %all-reduce.8.cloned.1.call-done = f32[384,2,128]{0,2,1:T(8,128)} async-done(((f32[384,2,128]{0,2,1:T(8,128)}), f32[384,2,128]{0,2,1:T(8,128)}) %all-reduce.8.cloned.1.call-update) | async-done | bytes 393232 | tf_op jit(solution)/shard_map/psum | solution.py:99
  407.7 1.0 multiply_reduce_fusion
  408.8 1.1 multiply_multiply_fusion
  411.8 114.2 %pmax.14 = f32[8,1,2,48]{3,2,0,1:T(2,128)S(1)} all-reduce(f32[8,1,2,48]{3,2,0,1:T(2,128)S(1)} %bitcast.134), channel_id=1, replica_groups=mesh['seq'=64,'tp'=8] {'seq'}, use_global_device_ids=true, to_apply=%region_6.0 | all-reduce | flops 768 | bytes 6144 | tf_op jit(solution)/shard_map/pmax | solution.py:127
  526.5 1.1 fusion.2
  528.0 219.4 %all-reduce.13 = (bf16[384,128]{1,0:T(8,128)(2,1)S(1)}, f32[8,1,2,48]{3,2,0,1:T(2,128)S(1)}) all-reduce(f32[384,128]{1,0:T(8,128)S(1)} %fusion.84, f32[8,1,2,48]{3,2,0,1:T(2,128)S(1)} %get-tuple-element.32), channel_id=1, replica_groups=mesh['seq'=64,'tp'=8] {'seq'}, use_global_device_ids=true, to_apply=%region_11.12 | all-reduce | flops 49920 | bytes 301056 | tf_op jit(solution)/shard_map/psum | solution.py:99
  747.3 74.5 %all-reduce.12.cloned.1.call-done = (f32[8,1,2,48,128]{4,3,2,0,1:T(8,128)}, f32[384,128]{1,0:T(8,128)}, f32[384,256]{1,0:T(8,128)}) async-done(((f32[8,1,2,48,128]{4,3,2,0,1:T(8,128)}, f32[384,128]{1,0:T(8,128)}, f32[384,256]{1,0:T(8,128)}), (f32[8,1,2,48,128]{4,3,2,0,1:T(8,128)}, f32[384,128]{1,0:T(8,128)}, f32[384,256]{1,0:T(8,128)})) %all-reduce.12.cloned.1.call-update) | async-done | bytes 983056 | tf_op jit(solution)/shard_map/psum | solution.py:129
  821.8 1.1 multiply_reduce_fusion.1
  822.9 1.1 multiply_bitcast_fusion
  824.0 0.8 fusion.25
  826.7 39.8 %psum.112 = f32[384,32]{0,1:T(8,128)S(1)} all-reduce(f32[384,32]{0,1:T(8,128)S(1)} %fusion.43), channel_id=1, replica_groups=mesh['seq'=64,'tp'=8] {'tp'}, use_global_device_ids=true, to_apply=%region_16.17 | all-reduce | flops 12288 | bytes 98304 | tf_op jit(solution)/shard_map/psum | solution.py:150
  866.5 110.1 %psum.113 = f32[384]{0:T(512)S(1)} all-reduce(f32[384]{0:T(512)S(1)} %get-tuple-element.21), channel_id=1, replica_groups=mesh['seq'=64,'tp'=8] {'seq'}, use_global_device_ids=true, to_apply=%region_18.19 | all-reduce | flops 384 | bytes 3072 | tf_op jit(solution)/shard_map/psum | solution.py:153
  976.7 1.4 fusion.63
  978.1 1.4 fusion.65
  979.6 295.4 %all-reduce.10.cloned.1.call-done = (f32[384,768]{1,0:T(8,128)}, f32[384,768]{1,0:T(8,128)}) async-done(((f32[384,768]{1,0:T(8,128)}, f32[384,768]{1,0:T(8,128)}), (f32[384,768]{1,0:T(8,128)}, f32[384,768]{1,0:T(8,128)})) %all-reduce.10.cloned.1.call-update) | async-done | bytes 2359312 | tf_op jit(solution)/shard_map/psum | solution.py:157
  1275.1 2.1 fusion.8
  1277.2 30.1 %psum.116 = f32[384,32]{0,1:T(8,128)S(1)} all-reduce(f32[384,32]{0,1:T(8,128)S(1)} %fusion.8), channel_id=1, replica_groups=mesh['seq'=64,'tp'=8] {'tp'}, use_global_device_ids=true, to_apply=%region_21.22 | all-reduce | flops 12288 | bytes 98304 | tf_op jit(solution)/shard_map/psum | solution.py:166
  1307.3 112.8 %psum.117 = f32[384]{0:T(512)S(1)} all-reduce(f32[384]{0:T(512)S(1)} %get-tuple-element.19), channel_id=1, replica_groups=mesh['seq'=64,'tp'=8] {'seq'}, use_global_device_ids=true, to_apply=%region_23.24 | all-reduce | flops 384 | bytes 3072 | tf_op jit(solution)/shard_map/psum | solution.py:169
  1421.9 1.7 fusion.1
  1423.5 1.6 fusion
  1425.1 148.8 %all-gather.2.cloned.1.call-done = bf16[384,2048]{0,1:T(8,128)(2,1)} async-done(((bf16[384,32]{0,1:T(8,128)(2,1)}), bf16[384,2048]{0,1:T(8,128)(2,1)}) %all-gather.2.cloned.1.call-update) | async-done | bytes 1572880 | tf_op jit(solution)/shard_map/all_gather | solution.py:174
  1573.9 2.2 fusion.93
  1576.1 109.6 %pmax.15 = f32[384]{0:T(512)S(1)} all-reduce(f32[384]{0:T(512)S(1)} %get-tuple-element.41), channel_id=1, replica_groups=mesh['seq'=64,'tp'=8] {'seq','tp'}, use_global_device_ids=true, to_apply=%region_25.26 | all-reduce | flops 384 | bytes 3072 | tf_op jit(solution)/shard_map/pmax | solution.py:179
  1685.8 112.0 %psum.118 = f32[384]{0:T(512)S(1)} all-reduce(f32[384]{0:T(512)S(1)} %exponential_reduce_fusion), channel_id=1, replica_groups=mesh['seq'=64,'tp'=8] {'seq'}, use_global_device_ids=true, to_apply=%region_27.28 | all-reduce | flops 384 | bytes 3072 | tf_op jit(solution)/shard_map/psum | solution.py:181
  1797.8 40.3 %psum.119 = f32[384]{0:T(512)S(1)} all-reduce(f32[384]{0:T(512)S(1)} %psum.118), channel_id=1, replica_groups=mesh['seq'=64,'tp'=8] {'tp'}, use_global_device_ids=true, to_apply=%region_28.29 | all-reduce | flops 384 | bytes 3072 | tf_op jit(solution)/shard_map/psum | solution.py:180
  1838.1 0.9 copy.35
  (101 shorter events, 8.8 us)
Async XLA Ops:
  7.2 1566.7 %copy-start = (bf16[2048,256]{1,0:T(8,128)(2,1)S(1)}, bf16[2048,256]{1,0:T(8,128)(2,1)}, u32[]{:S(2)}) copy-start(bf16[2048,256]{1,0:T(8,128)(2,1)} %param.35) | copy-start | bytes 3145732
  7.2 400.6 %all-reduce.8.cloned.1.call-start = ((), (), s32[]{:S(2)}) async-start(), calls=%async_computation | async-start | bytes 786432 | tf_op jit(solution)/shard_map/psum | solution.py:99
  132.7 689.1 %all-reduce.12.cloned.1.call-start = ((), (), s32[]{:S(2)}) async-start(), calls=%async_computation.3 | async-start | bytes 1966080 | tf_op jit(solution)/shard_map/psum | solution.py:129
  134.6 1.4 copy-start.12
  134.6 1.6 copy-start.1
  134.6 1.6 copy-start.8
  134.6 1.6 copy-start.9
  135.0 2.7 copy-start.7
  135.3 273.5 %copy-start.16 = (f32[128]{0:T(128)S(1)}, f32[128]{0:T(128)}, u32[]{:S(2)}) copy-start(f32[128]{0:T(128)} %param.27) | copy-start | bytes 1540
  410.4 1.0 copy-start.2
  411.4 115.0 %copy-start.3 = (bf16[8,256,128]{2,1,0:T(8,128)(2,1)S(1)}, bf16[8,256,128]{2,1,0:T(8,128)(2,1)}, u32[]{:S(2)}) copy-start(bf16[8,256,128]{2,1,0:T(8,128)(2,1)} %param.38) | copy-start | bytes 1572868
  526.5 1.2 copy-start.10
  527.6 295.3 %copy-start.13 = (f32[128]{0:T(128)S(1)}, f32[128]{0:T(128)}, u32[]{:S(2)}) copy-start(f32[128]{0:T(128)} %param.28) | copy-start | bytes 1540
  527.6 747.5 %all-reduce.10.cloned.1.call-start = ((), (), s32[]{:S(2)}) async-start(), calls=%async_computation.2 | async-start | bytes 4718592 | tf_op jit(solution)/shard_map/psum | solution.py:157
  822.9 2.5 copy-start.18
  825.4 1.0 copy-start.17
  825.4 1.0 copy-start.20
  826.0 150.7 %copy-start.5 = (bf16[32,768]{1,0:T(8,128)(2,1)S(1)}, bf16[32,768]{1,0:T(8,128)(2,1)}, u32[]{:S(2)}) copy-start(bf16[32,768]{1,0:T(8,128)(2,1)} %param.32) | copy-start | bytes 147460
  826.0 150.7 %copy-start.11 = (f32[32]{0:T(128)S(1)}, f32[32]{0:T(128)}, u32[]{:S(2)}) copy-start(f32[32]{0:T(128)} %param.30) | copy-start | bytes 388
  826.7 151.5 %copy-start.6 = (bf16[32,768]{1,0:T(8,128)(2,1)S(1)}, bf16[32,768]{1,0:T(8,128)(2,1)}, u32[]{:S(2)}) copy-start(bf16[32,768]{1,0:T(8,128)(2,1)} %param.31) | copy-start | bytes 147460
  979.5 295.5 %copy-start.19 = (bf16[768,32]{0,1:T(8,128)(2,1)S(1)}, bf16[768,32]{0,1:T(8,128)(2,1)}, u32[]{:S(2)}) copy-start(bf16[768,32]{0,1:T(8,128)(2,1)} %param.33) | copy-start | bytes 147460
  979.6 594.3 %all-gather.2.cloned.1.call-start = ((), (), s32[]{:S(2)}) async-start(), calls=%async_computation.1 | async-start | bytes 1597440 | tf_op jit(solution)/shard_map/all_gather | solution.py:174
  1275.0 145.0 %copy-start.14 = (f32[32]{0:T(128)S(1)}, f32[32]{0:T(128)}, u32[]{:S(2)}) copy-start(f32[32]{0:T(128)} %param.34) | copy-start | bytes 388
  1275.0 145.7 %copy-start.15 = (f32[8]{0:T(128)S(1)}, f32[8]{0:T(128)}, u32[]{:S(2)}) copy-start(f32[8]{0:T(128)} %param.36) | copy-start | bytes 100
  1275.0 146.0 %copy-start.21 = (s32[8]{0:T(128)S(1)}, s32[8]{0:T(128)}, u32[]{:S(2)}) copy-start(s32[8]{0:T(128)} %param.41) | copy-start | bytes 100
  1307.3 117.8 %copy-start.4 = (bf16[384,32]{0,1:T(8,128)(2,1)}, bf16[384,32]{0,1:T(8,128)(2,1)S(1)}, u32[]{:S(2)}) copy-start(bf16[384,32]{0,1:T(8,128)(2,1)S(1)} %get-tuple-element.20) | copy-start | bytes 73732
Sparse Core Ops, SparseCore 0:
  132.9 274.8 all-reduce.7
  527.7 294.0 all-reduce.11
  979.7 295.2 all-reduce.9
  1420.9 152.9 all-gather.1
